TPU v7x, 32 devices: a whole 2x2x4 slice. The times are simulated.
32 devices in a mesh: rows: 2 (over y), cols: 16 (over z, x, core).
Axes of the slice: x: 2, y: 2, z: 4, core: 2. Of those that a mesh axis runs over, the one named last changes fastest.
Arguments:
- eigvecs: float32 [1024, 2048], P('rows', 'cols'), may hold values from -6 to 6
- wy_packed: float32 [32, 128, 128], P(('rows', 'cols')), may hold values from -6 to 6
- slot_block: int32 [2, 8, 2], P('rows'), may hold values from 0 to 1, each once within a row
Outputs:
- transformed: float32 [1024, 2048], P('rows', 'cols')
Inputs may be any that keep to these rules, and one draw needn't show every extreme that they name: `slot_block`: for every group and level the 2 entries name each of 0 .. 1 once.
All inputs are finite; a program needn't handle non-finite values.
Results may differ from a plain program's by a relative error of at most 0.0003.
Values sent between devices are 32-bit elements; how exact they have to be, the bound alone decides.
A program may use at most 64 MiB of HBM per device.

v0:
```python
import jax
import jax.numpy as jnp
from jax import lax
from jax.sharding import PartitionSpec as P

LEVELS = 8


highest = lax.Precision.HIGHEST


def passed_along(value, axis, steps):
    count = lax.axis_size(axis)
    first, last = (max(0, -steps), min(count, count - steps))
    return lax.ppermute(value, axis, [(source, source + steps) for source in range(first, last)])


def unpack(packed):
    blocks, band_width = (packed.shape[0], packed.shape[1])
    flipped = jnp.swapaxes(packed, 1, 2)
    padded = jnp.pad(flipped, ((0, 0), (0, 0), (0, band_width + 1)))
    flattened = padded.reshape(blocks, band_width * (2 * band_width + 1))[
        :, : 2 * band_width * band_width
    ]
    return flattened.reshape(blocks, band_width, 2 * band_width)


def upper_inverse(upper):
    band_width = upper.shape[1]
    index_row = jnp.arange(band_width, dtype=jnp.int32)
    diag_values = jnp.diagonal(upper, axis1=1, axis2=2)
    identity = jnp.eye(band_width, dtype=upper.dtype)
    inverted = identity[None] * (1.0 / diag_values)[:, None, :]
    width = 1
    while width < band_width:
        same_new = index_row[:, None] // (2 * width) == index_row[None, :] // (2 * width)
        same_old = index_row[:, None] // width == index_row[None, :] // width
        selector = jnp.logical_and(same_new, jnp.logical_not(same_old)).astype(upper.dtype)
        corner = upper * selector[None]
        partial_block = jnp.einsum("nij,njk->nik", corner, inverted, precision=highest)
        inverted = inverted - jnp.einsum("nij,njk->nik", inverted, partial_block, precision=highest)
        width = 2 * width
    return inverted


def wy_factor(reflectors):
    band_width = reflectors.shape[1]
    gram_matrix = jnp.einsum("njr,nkr->njk", reflectors, reflectors, precision=highest)
    identity = jnp.eye(band_width, dtype=gram_matrix.dtype)
    triangle = jnp.triu(gram_matrix, 1) + 0.5 * gram_matrix * identity
    return upper_inverse(triangle)


def reflect(reflectors, factors, windows):
    projected = jnp.einsum("njr,nrc->njc", reflectors, windows, precision=highest)
    scaled = jnp.einsum("njk,nkc->njc", factors, projected, precision=highest)
    return windows - jnp.einsum("njr,njc->nrc", reflectors, scaled, precision=highest)


def per_device(eigvecs, wy_packed, slot_block):
    band_width = wy_packed.shape[1]
    row_count, col_count = eigvecs.shape
    per_level = row_count // (2 * band_width)
    orders = slot_block[0]
    payload = jnp.stack([wy_packed, wy_factor(unpack(wy_packed))], axis=1)
    gathered = lax.all_gather(payload, "cols", axis=0, tiled=True)
    current = eigvecs
    first_owner = lax.axis_index("rows") == 0
    positions = jnp.arange(per_level, dtype=jnp.int32)
    for level_index in range(LEVELS):
        pieces = gathered[level_index * per_level : (level_index + 1) * per_level]
        selector = (orders[level_index][:, None] == positions[None, :]).astype(jnp.float32)
        chosen = jnp.einsum("hp,pkij->hkij", selector, pieces, precision=highest)
        reflectors = unpack(chosen[:, 0])
        factors = chosen[:, 1]
        if level_index % 2 == 0:
            windows = current.reshape(per_level, 2 * band_width, col_count)
            current = reflect(reflectors, factors, windows).reshape(row_count, col_count)
        else:
            below = passed_along(current[:band_width], "rows", -1)
            extended = jnp.concatenate([current[band_width:], below], axis=0)
            windows = extended.reshape(per_level, 2 * band_width, col_count)
            result = reflect(reflectors, factors, windows).reshape(row_count, col_count)
            above = passed_along(result[row_count - band_width :], "rows", 1)
            middle = result[: row_count - band_width]
            top_rows = jnp.where(first_owner, current[:band_width], above)
            current = jnp.concatenate([top_rows, middle], axis=0)
    return current


def solution(mesh):
    placed = (P("rows", "cols"), P(("rows", "cols"), None, None), P("rows", None, None))
    return jax.shard_map(
        per_device, mesh=mesh, in_specs=placed, out_specs=P("rows", "cols"), check_vma=False
    )
```

profile of v0, /device:TPU:0, one launch (start us, length us, event | category | flops | bytes accessed | tf_op | source)
XLA Modules:
  0.0 122.0 jit_solution(6230743955057058136)
XLA Ops:
  6.6 0.9 copy.94
  8.7 1.2 %gather_fusion = f32[128]{0:T(128)S(1)} fusion(f32[128,128]{1,0:T(8,128)S(1)} %get-tuple-element.37, s32[128]{0:T(128)S(1)} %or_bitcast_fusion), kind=kCustom, calls=%fused_computation | custom fusion | bytes 2048 | tf_op jit(solution)/shard_map/jit(diagonal)/gather | solution.py:31
  14.3 44.0 %all-gather.2.cloned.1.call-done = f32[16,2,128,128]{3,2,1,0:T(8,128)} async-done(((f32[1,2,128,128]{3,2,1,0:T(8,128)}), f32[16,2,128,128]{3,2,1,0:T(8,128)}) %all-gather.2.cloned.1.call-update) | async-done | bytes 2097168 | tf_op jit(solution)/shard_map/all_gather | solution.py:66
  58.3 1.6 %fusion.170 = (f32[2,2,128,128]{3,2,1,0:T(8,128)S(1)}, f32[2,2,128,128]{3,2,1,0:T(8,128)S(1)}, f32[2,2,128,128]{3,2,1,0:T(8,128)S(1)}, f32[2,2,128,128]{3,2,1,0:...) fusion(f32[16,2,128,128]{3,2,1,0:T(8,128)} %all-gather.2.cloned, ...), kind=kLoop, calls=%fused_computation.262 | loop fusion | bytes 4194304 | tf_op jit(solution)/shard_map/slice | solution.py:71
  62.7 1.5 %collective-permute-start = (f32[128,128]{1,0:T(8,128)S(1)}, f32[128,128]{1,0:T(8,128)S(1)}, u32[]{:S(2)}, u32[]{:S(2)}) collective-permute-start(f32[128,128]{1,0:T(8,128)S(1)} %slice.247), channel_id=1, source_target_pairs={{16,0},{17,1},{18,2},{19,3},{20,4},{21,5},{22,6},{23,7},{24,8},{25... | collective-permute-start | bytes 196616 | tf_op jit(solution)/shard_map/ppermute | solution.py:15
  64.2 0.7 fusion.37
  65.6 0.7 fusion.33
  66.3 0.7 fusion.31
  67.1 0.7 fusion.29
  71.3 4.5 %collective-permute-start.1 = (f32[128,128]{1,0:T(8,128)S(1)}, f32[128,128]{1,0:T(8,128)S(1)}, u32[]{:S(2)}, u32[]{:S(2)}) collective-permute-start(f32[128,128]{1,0:T(8,128)S(1)} %slice.253), channel_id=1, source_target_pairs={{0,16},{1,17},{2,18},{3,19},{4,20},{5,21},{6,22},{7,23},{8,24},{9,... | collective-permute-start | bytes 196616 | tf_op jit(solution)/shard_map/ppermute | solution.py:15
  76.5 1.2 collective-permute-done.1
  79.0 1.3 %collective-permute-start.2 = (f32[128,128]{1,0:T(8,128)S(1)}, f32[128,128]{1,0:T(8,128)S(1)}, u32[]{:S(2)}, u32[]{:S(2)}) collective-permute-start(f32[128,128]{1,0:T(8,128)S(1)} %slice.259), channel_id=1, source_target_pairs={{16,0},{17,1},{18,2},{19,3},{20,4},{21,5},{22,6},{23,7},{24,8},{25... | collective-permute-start | bytes 196616 | tf_op jit(solution)/shard_map/ppermute | solution.py:15
  81.0 4.1 %collective-permute-done.2 = f32[128,128]{1,0:T(8,128)S(1)} collective-permute-done((f32[128,128]{1,0:T(8,128)S(1)}, f32[128,128]{1,0:T(8,128)S(1)}, u32[]{:S(2)}, u32[]{:S(2)}) %collective-permute-start.2) | collective-permute-done | bytes 65568 | tf_op jit(solution)/shard_map/ppermute | solution.py:15
  86.5 1.8 %collective-permute-start.3 = (f32[128,128]{1,0:T(8,128)S(1)}, f32[128,128]{1,0:T(8,128)S(1)}, u32[]{:S(2)}, u32[]{:S(2)}) collective-permute-start(f32[128,128]{1,0:T(8,128)S(1)} %slice.265), channel_id=1, source_target_pairs={{0,16},{1,17},{2,18},{3,19},{4,20},{5,21},{6,22},{7,23},{8,24},{9,... | collective-permute-start | bytes 196616 | tf_op jit(solution)/shard_map/ppermute | solution.py:15
  89.0 0.9 collective-permute-done.3
  91.3 1.3 %collective-permute-start.4 = (f32[128,128]{1,0:T(8,128)S(1)}, f32[128,128]{1,0:T(8,128)S(1)}, u32[]{:S(2)}, u32[]{:S(2)}) collective-permute-start(f32[128,128]{1,0:T(8,128)S(1)} %slice.271), channel_id=1, source_target_pairs={{16,0},{17,1},{18,2},{19,3},{20,4},{21,5},{22,6},{23,7},{24,8},{25... | collective-permute-start | bytes 196616 | tf_op jit(solution)/shard_map/ppermute | solution.py:15
  93.3 4.1 %collective-permute-done.4 = f32[128,128]{1,0:T(8,128)S(1)} collective-permute-done((f32[128,128]{1,0:T(8,128)S(1)}, f32[128,128]{1,0:T(8,128)S(1)}, u32[]{:S(2)}, u32[]{:S(2)}) %collective-permute-start.4) | collective-permute-done | bytes 65568 | tf_op jit(solution)/shard_map/ppermute | solution.py:15
  98.7 1.6 %collective-permute-start.5 = (f32[128,128]{1,0:T(8,128)S(1)}, f32[128,128]{1,0:T(8,128)S(1)}, u32[]{:S(2)}, u32[]{:S(2)}) collective-permute-start(f32[128,128]{1,0:T(8,128)S(1)} %slice.277), channel_id=1, source_target_pairs={{0,16},{1,17},{2,18},{3,19},{4,20},{5,21},{6,22},{7,23},{8,24},{9,... | collective-permute-start | bytes 196616 | tf_op jit(solution)/shard_map/ppermute | solution.py:15
  101.0 1.2 collective-permute-done.5
  103.5 1.3 %collective-permute-start.6 = (f32[128,128]{1,0:T(8,128)S(1)}, f32[128,128]{1,0:T(8,128)S(1)}, u32[]{:S(2)}, u32[]{:S(2)}) collective-permute-start(f32[128,128]{1,0:T(8,128)S(1)} %slice.283), channel_id=1, source_target_pairs={{16,0},{17,1},{18,2},{19,3},{20,4},{21,5},{22,6},{23,7},{24,8},{25... | collective-permute-start | bytes 196616 | tf_op jit(solution)/shard_map/ppermute | solution.py:15
  105.5 4.1 %collective-permute-done.6 = f32[128,128]{1,0:T(8,128)S(1)} collective-permute-done((f32[128,128]{1,0:T(8,128)S(1)}, f32[128,128]{1,0:T(8,128)S(1)}, u32[]{:S(2)}, u32[]{:S(2)}) %collective-permute-start.6) | collective-permute-done | bytes 65568 | tf_op jit(solution)/shard_map/ppermute | solution.py:15
  111.0 1.6 %collective-permute-start.7 = (f32[128,128]{1,0:T(8,128)S(1)}, f32[128,128]{1,0:T(8,128)S(1)}, u32[]{:S(2)}, u32[]{:S(2)}) collective-permute-start(f32[128,128]{1,0:T(8,128)S(1)} %slice.289), channel_id=1, source_target_pairs={{0,16},{1,17},{2,18},{3,19},{4,20},{5,21},{6,22},{7,23},{8,24},{9,... | collective-permute-start | bytes 196616 | tf_op jit(solution)/shard_map/ppermute | solution.py:15
  112.6 1.9 %collective-permute-done.7 = f32[128,128]{1,0:T(8,128)S(1)} collective-permute-done((f32[128,128]{1,0:T(8,128)S(1)}, f32[128,128]{1,0:T(8,128)S(1)}, u32[]{:S(2)}, u32[]{:S(2)}) %collective-permute-start.7) | collective-permute-done | bytes 65568 | tf_op jit(solution)/shard_map/ppermute | solution.py:15
  114.5 0.7 pad_maximum_fusion.7
  (131 shorter events, 23.8 us)
Async XLA Ops:
  6.5 51.8 %all-gather.2.cloned.1.call-start = ((), (), s32[]{:S(2)}) async-start(), calls=%async_computation | async-start | bytes 2228224 | tf_op jit(solution)/shard_map/all_gather | solution.py:66
  8.4 4.9 %copy-start.1 = (f32[1,128,128]{2,1,0:T(8,128)S(1)}, f32[1,128,128]{2,1,0:T(8,128)}, u32[]{:S(2)}) copy-start(f32[1,128,128]{2,1,0:T(8,128)} %param.4) | copy-start | bytes 196612
  8.7 5.3 %copy-start.2 = (s32[1,8,2]{1,2,0:T(2,128)S(1)}, s32[1,8,2]{1,2,0:T(2,128)}, u32[]{:S(2)}) copy-start(s32[1,8,2]{1,2,0:T(2,128)} %param.5) | copy-start | bytes 196
  60.0 1.4 %copy-start = (f32[512,128]{1,0:T(8,128)S(1)}, f32[512,128]{1,0:T(8,128)}, u32[]{:S(2)}) copy-start(f32[512,128]{1,0:T(8,128)} %param.3) | copy-start | bytes 786436
  62.7 7.2 %collective-permute-start = (f32[128,128]{1,0:T(8,128)S(1)}, f32[128,128]{1,0:T(8,128)S(1)}, u32[]{:S(2)}, u32[]{:S(2)}) collective-permute-start(f32[128,128]{1,0:T(8,128)S(1)} %slice.247), channel_id=1, source_target_pairs={{16,0},{17,1},{18,2},{19,3},{20,4},{21,5},{22,6},{23,7},{24,8},{25... | collective-permute-start | bytes 196616 | tf_op jit(solution)/shard_map/ppermute | solution.py:15
  71.3 6.4 %collective-permute-start.1 = (f32[128,128]{1,0:T(8,128)S(1)}, f32[128,128]{1,0:T(8,128)S(1)}, u32[]{:S(2)}, u32[]{:S(2)}) collective-permute-start(f32[128,128]{1,0:T(8,128)S(1)} %slice.253), channel_id=1, source_target_pairs={{0,16},{1,17},{2,18},{3,19},{4,20},{5,21},{6,22},{7,23},{8,24},{9,... | collective-permute-start | bytes 196616 | tf_op jit(solution)/shard_map/ppermute | solution.py:15
  79.0 6.2 %collective-permute-start.2 = (f32[128,128]{1,0:T(8,128)S(1)}, f32[128,128]{1,0:T(8,128)S(1)}, u32[]{:S(2)}, u32[]{:S(2)}) collective-permute-start(f32[128,128]{1,0:T(8,128)S(1)} %slice.259), channel_id=1, source_target_pairs={{16,0},{17,1},{18,2},{19,3},{20,4},{21,5},{22,6},{23,7},{24,8},{25... | collective-permute-start | bytes 196616 | tf_op jit(solution)/shard_map/ppermute | solution.py:15
  86.5 3.5 %collective-permute-start.3 = (f32[128,128]{1,0:T(8,128)S(1)}, f32[128,128]{1,0:T(8,128)S(1)}, u32[]{:S(2)}, u32[]{:S(2)}) collective-permute-start(f32[128,128]{1,0:T(8,128)S(1)} %slice.265), channel_id=1, source_target_pairs={{0,16},{1,17},{2,18},{3,19},{4,20},{5,21},{6,22},{7,23},{8,24},{9,... | collective-permute-start | bytes 196616 | tf_op jit(solution)/shard_map/ppermute | solution.py:15
  91.3 6.2 %collective-permute-start.4 = (f32[128,128]{1,0:T(8,128)S(1)}, f32[128,128]{1,0:T(8,128)S(1)}, u32[]{:S(2)}, u32[]{:S(2)}) collective-permute-start(f32[128,128]{1,0:T(8,128)S(1)} %slice.271), channel_id=1, source_target_pairs={{16,0},{17,1},{18,2},{19,3},{20,4},{21,5},{22,6},{23,7},{24,8},{25... | collective-permute-start | bytes 196616 | tf_op jit(solution)/shard_map/ppermute | solution.py:15
  98.7 3.5 %collective-permute-start.5 = (f32[128,128]{1,0:T(8,128)S(1)}, f32[128,128]{1,0:T(8,128)S(1)}, u32[]{:S(2)}, u32[]{:S(2)}) collective-permute-start(f32[128,128]{1,0:T(8,128)S(1)} %slice.277), channel_id=1, source_target_pairs={{0,16},{1,17},{2,18},{3,19},{4,20},{5,21},{6,22},{7,23},{8,24},{9,... | collective-permute-start | bytes 196616 | tf_op jit(solution)/shard_map/ppermute | solution.py:15
  103.5 6.2 %collective-permute-start.6 = (f32[128,128]{1,0:T(8,128)S(1)}, f32[128,128]{1,0:T(8,128)S(1)}, u32[]{:S(2)}, u32[]{:S(2)}) collective-permute-start(f32[128,128]{1,0:T(8,128)S(1)} %slice.283), channel_id=1, source_target_pairs={{16,0},{17,1},{18,2},{19,3},{20,4},{21,5},{22,6},{23,7},{24,8},{25... | collective-permute-start | bytes 196616 | tf_op jit(solution)/shard_map/ppermute | solution.py:15
  111.0 3.5 %collective-permute-start.7 = (f32[128,128]{1,0:T(8,128)S(1)}, f32[128,128]{1,0:T(8,128)S(1)}, u32[]{:S(2)}, u32[]{:S(2)}) collective-permute-start(f32[128,128]{1,0:T(8,128)S(1)} %slice.289), channel_id=1, source_target_pairs={{0,16},{1,17},{2,18},{3,19},{4,20},{5,21},{6,22},{7,23},{8,24},{9,... | collective-permute-start | bytes 196616 | tf_op jit(solution)/shard_map/ppermute | solution.py:15
Sparse Core Ops, SparseCore 0:
  14.1 44.1 all-gather.1
where the time goes:
time: 122 us
  waiting for transfers between devices  61.6 us (50%)
  matrix products  19.1 us (16%)
  starting transfers between devices  14.8 us (12%)
  between operations  14.4 us (12%)
  local copies, waits for them, and re-layouts  10.5 us (9%)
  other arithmetic  1.59 us (1%)
    all_gather x1, waiting for transfers between devices, per_device(): gathered = lax.all_gather(payload, 'cols', axis=0, tiled=True)  44 us
    ppermute x8, waiting for transfers between devices, passed_along(): lax.ppermute(value, axis, [(source, source + steps) for source in range(f...  17.6 us
    ppermute x8, starting transfers between devices, passed_along(): lax.ppermute(value, axis, [(source, source + steps) for source in range(f...  14.8 us
    dot_general x8, matrix products, per_device(): chosen = jnp.einsum('hp,pkij->hkij', selector, pieces, precision=highest)  5.68 us
    dot_general x8, matrix products, reflect(): jnp.einsum('njr,njc->nrc', reflectors, scaled, precision=highest)  4.71 us
    reshape x9, local copies, waits for them, and re-layouts, unpack(): padded.reshape(blocks, band_width * (2 * band_width + 1))  4.47 us
    dot_general x8, matrix products, reflect(): jnp.einsum('njr,nrc->njc', reflectors, windows, precision=highest)  3.1 us
  transfers between devices with their start and end apart: 9, of which 8 were waited for; matrix products, arithmetic and copies ran while one was open for 8% of the time, Pallas kernels for 0%

commit v1 on v0

v1 whole, which is shorter than its diff:
```python
import functools

import jax
import jax.numpy as jnp
from jax import lax
from jax.experimental import pallas as pl
from jax.experimental.pallas import tpu as pltpu
from jax.sharding import PartitionSpec as P

MESH = pl.DeviceIdType.MESH
F32 = jnp.float32
BF16 = jnp.bfloat16
NN = (((1,), (0,)), ((), ()))
NT = (((1,), (1,)), ((), ()))


def split(value):
    high = value.astype(BF16)
    low = (value - high.astype(F32)).astype(BF16)
    return high, low


def product(a, b, dims=NN):
    dot = functools.partial(lax.dot_general, dimension_numbers=dims, preferred_element_type=F32)
    return dot(a[0], b[0]) + (dot(a[0], b[1]) + dot(a[1], b[0]))


def exact(a, b, dims=NN):
    return lax.dot_general(
        a, b, dims, precision=lax.Precision.HIGHEST, preferred_element_type=F32
    )


def kernel(
    levels, n_rows, n_z, slot_ref, eig_ref, wy_ref, out_ref,
    wg, tg, xt, up_send, up_recv, down_send, down_recv,
    recv_sem, send_sem, own_sem, up_sem, down_sem,
):
    band = wy_ref.shape[1]
    chunks = eig_ref.shape[0] // band
    per_level = chunks // 2
    g = lax.axis_index("rows")
    c = lax.axis_index("cols")
    z, x, k = c // 4, (c // 2) % 2, c % 2
    x_partner = z * 4 + (1 - x) * 2 + k
    core_partner = z * 4 + x * 2 + (1 - k)
    z_mates = [((z + d) % n_z) * 4 + x * 2 + k for d in range(1, n_z)]
    has_above = g > 0
    has_below = g < n_rows - 1
    gathered = (wg, tg)

    barrier = pltpu.get_barrier_semaphore()
    for other in z_mates + [x_partner, core_partner]:
        pl.semaphore_signal(barrier, inc=1, device_id={"cols": other}, device_id_type=MESH)

    @pl.when(has_above)
    def _():
        pl.semaphore_signal(barrier, inc=1, device_id={"rows": g - 1}, device_id_type=MESH)

    @pl.when(has_below)
    def _():
        pl.semaphore_signal(barrier, inc=1, device_id={"rows": g + 1}, device_id_type=MESH)

    def block_copy(kind, block, target, sem):
        return pltpu.make_async_remote_copy(
            src_ref=gathered[kind].at[block],
            dst_ref=gathered[kind].at[block],
            send_sem=sem,
            recv_sem=recv_sem.at[kind, block],
            device_id={"cols": target},
            device_id_type=MESH,
        )

    def to_x(kind, zz, xx):
        return block_copy(kind, zz * 4 + xx * 2 + k, x_partner, send_sem.at[kind, zz * 2 + xx, 0])

    def to_core(kind, zz, xx):
        return block_copy(
            kind, zz * 4 + xx * 2 + k, core_partner, send_sem.at[kind, zz * 2 + xx, 1]
        )

    def to_z(kind, at):
        return block_copy(kind, c, z_mates[at], own_sem.at[kind, at])

    def send_own(kind):
        for at in range(n_z - 1):
            to_z(kind, at).start()
        to_x(kind, z, x).start()
        to_core(kind, z, x).start()

    def relay_z(kind, zz):
        @pl.when(z != zz)
        def _():
            to_x(kind, zz, x).wait_recv()
            to_x(kind, zz, x).start()
            to_core(kind, zz, x).start()

    def relay_x(kind, zz):
        to_core(kind, zz, 1 - x).wait_recv()
        to_core(kind, zz, 1 - x).start()

    sheared = pltpu.roll(jnp.transpose(wy_ref[0]), 0, 1, stride=1, stride_axis=0)
    wg[c] = sheared
    pl.semaphore_wait(
        barrier, n_z + 1 + has_above.astype(jnp.int32) + has_below.astype(jnp.int32)
    )
    send_own(0)

    for i in range(chunks):
        xt[i] = jnp.transpose(eig_ref[i * band : (i + 1) * band, :])

    row = lax.broadcasted_iota(jnp.int32, (band, band), 0)
    col = lax.broadcasted_iota(jnp.int32, (band, band), 1)
    upper = col >= row
    zero = jnp.zeros((band, band), F32)

    def spread(w):
        return jnp.concatenate([jnp.where(upper, w, zero), jnp.where(upper, zero, w)], axis=1)

    mine = spread(sheared)
    gram = exact(mine, mine, NT)
    diagonal = row == col
    on_diagonal = jnp.where(diagonal, 0.5 * gram, zero)
    by_row = 1.0 / jnp.sum(on_diagonal, axis=1, keepdims=True)
    by_col = 1.0 / jnp.sum(on_diagonal, axis=0, keepdims=True)
    strict = jnp.where(col > row, gram, zero)
    pairs = jnp.where(row // 2 == col // 2, strict, zero)
    inverse = jnp.where(diagonal, by_row, zero) - pairs * by_row * by_col
    width = 2
    while width < band:
        factor = 4 if width * 4 <= band else 2
        wide = width * factor
        inside = (row // wide == col // wide) & (row // width != col // width)
        corner = jnp.where(inside, strict, zero)
        nilpotent = exact(inverse, corner)
        stepped = inverse - exact(nilpotent, inverse)
        if factor == 4:
            stepped = stepped + exact(exact(nilpotent, nilpotent), stepped)
        inverse = stepped
        width = wide
        if width == 32:
            for zz in range(n_z):
                relay_z(0, zz)
    tg[c] = inverse
    send_own(1)
    for zz in range(n_z):
        relay_x(0, zz)
    for zz in range(n_z):
        relay_z(1, zz)

    def row_copy(src, dst, sem, at, target):
        return pltpu.make_async_remote_copy(
            src_ref=src.at[at],
            dst_ref=dst.at[at],
            send_sem=sem.at[0, at],
            recv_sem=sem.at[1, at],
            device_id={"rows": target},
            device_id_type=MESH,
        )

    def go_up(at):
        return row_copy(up_send, up_recv, up_sem, at, g - 1)

    def go_down(at):
        return row_copy(down_send, down_recv, down_sem, at, g + 1)

    def reflected(operators, top, bottom):
        z_parts, v_parts = operators
        pair = jnp.concatenate([top, bottom], axis=1)
        projected = product(split(pair), z_parts, NT)
        return pair - product(split(projected), v_parts)

    for level in range(levels):
        zz, xx = level // 2, level % 2
        for kind in range(2):
            other = 4 * zz + 2 * xx + 1 - k
            if kind == 1:
                @pl.when(x != xx)
                def _():
                    relay_x(1, zz)
            block_copy(kind, other, core_partner, send_sem.at[0, 0, 0]).wait_recv()
        stored = [(wg[level * per_level + s], tg[level * per_level + s]) for s in range(per_level)]
        operators = []
        for h in range(per_level):
            first = slot_ref[0, level, h] == 0
            w = jnp.where(first, stored[0][0], stored[1][0])
            t = jnp.where(first, stored[0][1], stored[1][1])
            v_parts = split(spread(w))
            z_parts = split(product(split(t), v_parts))
            operators.append((z_parts, v_parts))
        if level % 2 == 0:
            for h in range(per_level):
                new = reflected(operators[h], xt[2 * h], xt[2 * h + 1])
                xt[2 * h] = new[:, :band]
                xt[2 * h + 1] = new[:, band:]
        else:
            at = level // 2

            @pl.when(has_above)
            def _():
                up_send[at] = xt[0]
                go_up(at).start()

            for h in range(per_level - 1):
                new = reflected(operators[h], xt[2 * h + 1], xt[2 * h + 2])
                xt[2 * h + 1] = new[:, :band]
                xt[2 * h + 2] = new[:, band:]

            @pl.when(has_below)
            def _():
                go_up(at).wait_recv()

            @pl.when(jnp.logical_not(has_below))
            def _():
                up_recv[at] = zero

            new = reflected(operators[per_level - 1], xt[chunks - 1], up_recv[at])
            xt[chunks - 1] = new[:, :band]

            @pl.when(has_below)
            def _():
                down_send[at] = new[:, band:]
                go_down(at).start()

            @pl.when(has_above)
            def _():
                go_down(at).wait_recv()
                xt[0] = down_recv[at]

    for i in range(chunks):
        out_ref[i * band : (i + 1) * band, :] = jnp.transpose(xt[i])

    for kind in range(2):
        for at in range(n_z - 1):
            to_z(kind, at).wait_send()
        for zz in range(n_z):
            to_x(kind, zz, x).wait_send()
            for xx in range(2):
                to_core(kind, zz, xx).wait_send()
    for at in range(levels // 2):
        @pl.when(has_above)
        def _():
            go_up(at).wait_send()

        @pl.when(has_below)
        def _():
            go_down(at).wait_send()


def per_device(n_rows, n_cols, eigvecs, wy_packed, slot_block):
    band = wy_packed.shape[1]
    levels, per_level = slot_block.shape[1:]
    n_z = n_cols // 4
    assert n_cols == levels * per_level and n_cols % 4 == 0
    assert wy_packed.shape[0] == 1 and per_level == 2
    tile = (band, eigvecs.shape[1])
    blocks = pltpu.VMEM((n_cols, band, band), F32)
    slots = pltpu.VMEM((levels // 2,) + tile, F32)
    vmem = pl.BlockSpec(memory_space=pltpu.VMEM)
    return pl.pallas_call(
        functools.partial(kernel, levels, n_rows, n_z),
        out_shape=jax.ShapeDtypeStruct(eigvecs.shape, F32),
        in_specs=[pl.BlockSpec(memory_space=pltpu.SMEM), vmem, vmem],
        out_specs=vmem,
        scratch_shapes=[
            blocks,
            blocks,
            pltpu.VMEM((eigvecs.shape[0] // band,) + tile, F32),
            slots,
            slots,
            slots,
            slots,
            pltpu.SemaphoreType.DMA((2, n_cols)),
            pltpu.SemaphoreType.DMA((2, n_cols // 2, 2)),
            pltpu.SemaphoreType.DMA((2, n_z - 1)),
            pltpu.SemaphoreType.DMA((2, levels // 2)),
            pltpu.SemaphoreType.DMA((2, levels // 2)),
        ],
        compiler_params=pltpu.CompilerParams(collective_id=0, has_side_effects=True),
    )(slot_block, eigvecs, wy_packed)


def solution(mesh):
    placed = (P("rows", "cols"), P(("rows", "cols"), None, None), P("rows", None, None))
    return jax.shard_map(
        functools.partial(per_device, mesh.shape["rows"], mesh.shape["cols"]),
        mesh=mesh, in_specs=placed, out_specs=P("rows", "cols"), check_vma=False,
    )
```

time: 122 us -> 60.8 us (0.50)
  the two profiles are of different devices: /device:TPU:0 before, /device:TPU:14 now
where the time goes in v1:
time: 60.8 us; the launch traced here: 60.6 us
  Pallas kernels  57.6 us (95%)
  local copies, waits for them, and re-layouts  3.01 us (5%)
    pallas_call x1, Pallas kernels, per_device(): pl.pallas_call(functools.partial(kernel, levels, n_rows, n_z), out_shape=...  57.6 us
    unnamed x2, local copies, waits for them, and re-layouts  3.01 us

profile of v1, /device:TPU:14, one launch (start us, length us, event | category | flops | bytes accessed | tf_op | source)
XLA Modules:
  0.0 60.6 jit_solution(6181772827882901803)
XLA Ops:
  0.0 1.3 %copy.4.slot_ref = s32[1,8,2]{2,1,0:T(8,128)} copy(s32[1,8,2]{1,2,0:T(2,128)} %param.5) | data formatting | bytes 128 | tf_op args[2]
  1.3 57.6 %shard_map.37 = f32[512,128]{1,0:T(8,128)} custom-call(s32[1,8,2]{2,1,0:T(8,128)} %copy.4.slot_ref, f32[512,128]{1,0:T(8,128)} %eig_ref.1, f32[1,128,128]{2,1,0:T(8,128)} %wy_ref.1), custom_call_target="tpu_custom_call" | custom-call | tf_op jit(solution)/shard_map/pallas_call | solution.py:260
  58.9 1.7 %copy.6 = f32[512,128]{1,0:T(8,128)} copy(f32[512,128]{1,0:T(8,128)} %shard_map.37) | data formatting | bytes 524288

commit v2 on v1

v2 whole, which is shorter than its diff:
```python
import functools

import jax
import jax.numpy as jnp
from jax import lax
from jax.experimental import pallas as pl
from jax.experimental.pallas import tpu as pltpu
from jax.sharding import PartitionSpec as P

MESH = pl.DeviceIdType.MESH
F32 = jnp.float32
BF16 = jnp.bfloat16
NN = (((1,), (0,)), ((), ()))
NT = (((1,), (1,)), ((), ()))


def split(value):
    high = value.astype(BF16)
    low = (value - high.astype(F32)).astype(BF16)
    return high, low


def product(a, b, dims=NN):
    dot = functools.partial(lax.dot_general, dimension_numbers=dims, preferred_element_type=F32)
    return dot(a[0], b[0]) + (dot(a[0], b[1]) + dot(a[1], b[0]))


def inverses(grams, multiply):
    band = grams[0].shape[0]
    row = lax.broadcasted_iota(jnp.int32, (band, band), 0)
    col = lax.broadcasted_iota(jnp.int32, (band, band), 1)
    zero = jnp.zeros((band, band), F32)
    diagonal = row == col
    stricts, found = [], []
    for gram in grams:
        on_diagonal = jnp.where(diagonal, 0.5 * gram, zero)
        by_row = 1.0 / jnp.sum(on_diagonal, axis=1, keepdims=True)
        by_col = 1.0 / jnp.sum(on_diagonal, axis=0, keepdims=True)
        strict = jnp.where(col > row, gram, zero)
        pairs = jnp.where(row // 2 == col // 2, strict, zero)
        stricts.append(strict)
        found.append(jnp.where(diagonal, by_row, zero) - pairs * by_row * by_col)
    width = 2
    while width < band:
        factor = 4 if width * 4 <= band else 2
        wide = width * factor
        inside = (row // wide == col // wide) & (row // width != col // width)
        corners = [jnp.where(inside, strict, zero) for strict in stricts]
        powers = [multiply(a, b) for a, b in zip(found, corners)]
        firsts = [multiply(n, a) for n, a in zip(powers, found)]
        found = [a - b for a, b in zip(found, firsts)]
        if factor == 4:
            squares = [multiply(n, n) for n in powers]
            seconds = [multiply(n, a) for n, a in zip(squares, found)]
            found = [a + b for a, b in zip(found, seconds)]
        width = wide
    return found


def fast(a, b):
    return product(split(a), split(b))


def kernel(
    levels, n_rows, n_z, slot_ref, eig_ref, wy_ref, out_ref,
    wg, xt, ops, half_send, above, up_send, up_recv, down_send, down_recv,
    recv_sem, send_sem, own_sem, up_sem, down_sem, half_sem, side_sem,
):
    band = wy_ref.shape[1]
    chunks = eig_ref.shape[0] // band
    per_level = chunks // 2
    rounds = levels // 2
    g = lax.axis_index("rows")
    c = lax.axis_index("cols")
    z, x, k = c // 4, (c // 2) % 2, c % 2
    x_partner = z * 4 + (1 - x) * 2 + k
    core_partner = z * 4 + x * 2 + (1 - k)
    z_mates = [((z + d) % n_z) * 4 + x * 2 + k for d in range(1, n_z)]
    has_above = g > 0
    has_below = g < n_rows - 1

    barrier = pltpu.get_barrier_semaphore()
    for other in z_mates + [x_partner, core_partner]:
        pl.semaphore_signal(barrier, inc=1, device_id={"cols": other}, device_id_type=MESH)

    @pl.when(has_above)
    def _():
        pl.semaphore_signal(barrier, inc=1, device_id={"rows": g - 1}, device_id_type=MESH)

    @pl.when(has_below)
    def _():
        pl.semaphore_signal(barrier, inc=1, device_id={"rows": g + 1}, device_id_type=MESH)

    def block_copy(block, target, sem):
        return pltpu.make_async_remote_copy(
            src_ref=wg.at[block],
            dst_ref=wg.at[block],
            send_sem=sem,
            recv_sem=recv_sem.at[block],
            device_id={"cols": target},
            device_id_type=MESH,
        )

    def to_x(zz, xx):
        return block_copy(zz * 4 + xx * 2 + k, x_partner, send_sem.at[zz * 2 + xx, 0])

    def to_core(zz, xx):
        return block_copy(zz * 4 + xx * 2 + k, core_partner, send_sem.at[zz * 2 + xx, 1])

    def to_z(at):
        return block_copy(c, z_mates[at], own_sem.at[at])

    def relay_x(zz):
        to_core(zz, 1 - x).wait_recv()
        to_core(zz, 1 - x).start()

    def wait_core(zz):
        for xx in range(2):
            block_copy(zz * 4 + xx * 2 + 1 - k, core_partner, send_sem.at[0, 0]).wait_recv()

    def row_copy(src, dst, sem, at, target):
        return pltpu.make_async_remote_copy(
            src_ref=src.at[at],
            dst_ref=dst.at[at],
            send_sem=sem.at[0, at],
            recv_sem=sem.at[1, at],
            device_id={"rows": target},
            device_id_type=MESH,
        )

    def go_up(at):
        return row_copy(up_send, up_recv, up_sem, at, g - 1)

    def go_down(at):
        return row_copy(down_send, down_recv, down_sem, at, g + 1)

    half = band // 2

    def half_down(at):
        return pltpu.make_async_remote_copy(
            src_ref=half_send.at[at],
            dst_ref=above.at[at, pl.ds(k * half, half)],
            send_sem=half_sem.at[0, at],
            recv_sem=half_sem.at[1, at],
            device_id={"rows": g + 1},
            device_id_type=MESH,
        )

    def half_side(at):
        return pltpu.make_async_remote_copy(
            src_ref=above.at[at, pl.ds(k * half, half)],
            dst_ref=above.at[at, pl.ds(k * half, half)],
            send_sem=side_sem.at[0, at],
            recv_sem=side_sem.at[1, at],
            device_id={"cols": core_partner},
            device_id_type=MESH,
        )

    def send_half(at):
        level = 2 * at + 1
        first = slot_ref[0, level, per_level - 1] == 0
        rows = pl.ds(k * half, half)
        half_send[at] = jnp.where(
            first, wg[level * per_level, rows], wg[level * per_level + 1, rows]
        )
        half_down(at).start()

    wg[c] = pltpu.roll(jnp.transpose(wy_ref[0]), 0, 1, stride=1, stride_axis=0)
    pl.semaphore_wait(
        barrier, n_z + 1 + has_above.astype(jnp.int32) + has_below.astype(jnp.int32)
    )
    for at in range(n_z - 1):
        to_z(at).start()
    to_x(z, x).start()
    to_core(z, x).start()

    @pl.when(jnp.logical_not(has_above))
    def _():
        above[...] = jnp.zeros_like(above)
        down_recv[...] = jnp.zeros_like(down_recv)

    @pl.when(jnp.logical_not(has_below))
    def _():
        up_recv[...] = jnp.zeros_like(up_recv)

    for i in range(chunks):
        xt[i] = jnp.transpose(eig_ref[i * band : (i + 1) * band, :])

    row = lax.broadcasted_iota(jnp.int32, (band, band), 0)
    col = lax.broadcasted_iota(jnp.int32, (band, band), 1)
    upper = col >= row
    zero = jnp.zeros((band, band), F32)

    def spread(w):
        return jnp.concatenate([jnp.where(upper, w, zero), jnp.where(upper, zero, w)], axis=1)

    def chosen(level, h):
        first = slot_ref[0, level, h] == 0
        return jnp.where(first, wg[level * per_level], wg[level * per_level + 1])

    def prepare(sheared, places):
        v_parts = [split(spread(w)) for w in sheared]
        grams = [product(v, v, NT) for v in v_parts]
        factors = inverses(grams, fast)
        for place, v, t in zip(places, v_parts, factors):
            z_parts = split(product(split(t), v))
            ops[place, 0] = z_parts[0]
            ops[place, 1] = z_parts[1]
            ops[place, 2] = v[0]
            ops[place, 3] = v[1]

    def reflected(place, top, bottom):
        pair = jnp.concatenate([top, bottom], axis=1)
        projected = product(split(pair), (ops[place, 0], ops[place, 1]), NT)
        new = pair - product(split(projected), (ops[place, 2], ops[place, 3]))
        return new[:, :band], new[:, band:]

    for zz in range(n_z):
        @pl.when(z != zz)
        def _():
            to_x(zz, x).wait_recv()
            to_x(zz, x).start()
            to_core(zz, x).start()

    relay_x(0)
    wait_core(0)

    @pl.when(has_below)
    def _():
        send_half(0)

    prepare([chosen(0, 0), chosen(0, 1)], [3, 4])

    def both_levels(at, carry):
        for h in range(per_level):
            xt[2 * h], xt[2 * h + 1] = reflected(3 + h, xt[2 * h], xt[2 * h + 1])

        @pl.when(has_above)
        def _():
            up_send[at] = xt[0]
            go_up(at).start()

        @pl.when(has_below)
        def _():
            down_send[at] = xt[chunks - 1]
            go_down(at).start()

        @pl.when(at < rounds - 1)
        def _():
            relay_x(at + 1)
            wait_core(at + 1)

            @pl.when(has_below)
            def _():
                send_half(at + 1)

        @pl.when(has_above)
        def _():
            half_down(at).wait_recv()
            half_side(at).start()
            half_side(at).wait_recv()

        odd, even = 2 * at + 1, (2 * at + 2) % levels
        prepare(
            [chosen(odd, 0), chosen(odd, 1), above[at], chosen(even, 0), chosen(even, 1)],
            [0, 1, 2, 3, 4],
        )
        xt[1], xt[2] = reflected(0, xt[1], xt[2])

        @pl.when(has_below)
        def _():
            go_up(at).wait_recv()

        @pl.when(has_above)
        def _():
            go_down(at).wait_recv()

        last, _ = reflected(1, xt[chunks - 1], up_recv[at])
        _, first = reflected(2, down_recv[at], xt[0])
        xt[chunks - 1] = last
        xt[0] = jnp.where(has_above, first, xt[0])
        return carry

    lax.fori_loop(0, rounds, both_levels, 0)

    for i in range(chunks):
        out_ref[i * band : (i + 1) * band, :] = jnp.transpose(xt[i])

    for at in range(n_z - 1):
        to_z(at).wait_send()
    for zz in range(n_z):
        to_x(zz, x).wait_send()
        for xx in range(2):
            to_core(zz, xx).wait_send()
    for at in range(rounds):
        @pl.when(has_above)
        def _():
            go_up(at).wait_send()
            half_side(at).wait_send()

        @pl.when(has_below)
        def _():
            go_down(at).wait_send()
            half_down(at).wait_send()


def per_device(n_rows, n_cols, eigvecs, wy_packed, slot_block):
    band = wy_packed.shape[1]
    rows, cols = eigvecs.shape
    levels, per_level = slot_block.shape[1:]
    n_z = n_cols // 4
    rounds = levels // 2
    assert n_cols == levels * per_level and n_z == rounds
    assert wy_packed.shape[0] == 1 and per_level == 2 and rows == 4 * band
    blocks = pltpu.VMEM((rounds, band, band), F32)
    slots = pltpu.VMEM((rounds, cols, band), F32)
    vmem = pl.BlockSpec(memory_space=pltpu.VMEM)
    in_order = pltpu.SemaphoreType.DMA((2, rounds))
    return pl.pallas_call(
        functools.partial(kernel, levels, n_rows, n_z),
        out_shape=jax.ShapeDtypeStruct(eigvecs.shape, F32),
        in_specs=[pl.BlockSpec(memory_space=pltpu.SMEM), vmem, vmem],
        out_specs=vmem,
        scratch_shapes=[
            pltpu.VMEM((n_cols, band, band), F32),
            pltpu.VMEM((rows // band, cols, band), F32),
            pltpu.VMEM((5, 4, band, 2 * band), BF16),
            pltpu.VMEM((rounds, band // 2, band), F32),
            blocks,
            slots,
            slots,
            slots,
            slots,
            pltpu.SemaphoreType.DMA((n_cols,)),
            pltpu.SemaphoreType.DMA((n_cols // 2, 2)),
            pltpu.SemaphoreType.DMA((n_z - 1,)),
            in_order,
            in_order,
            in_order,
            in_order,
        ],
        compiler_params=pltpu.CompilerParams(collective_id=0, has_side_effects=True),
    )(slot_block, eigvecs, wy_packed)


def solution(mesh):
    placed = (P("rows", "cols"), P(("rows", "cols"), None, None), P("rows", None, None))
    return jax.shard_map(
        functools.partial(per_device, mesh.shape["rows"], mesh.shape["cols"]),
        mesh=mesh, in_specs=placed, out_specs=P("rows", "cols"), check_vma=False,
    )
```

time: 60.8 us -> 44.9 us (0.74)
  the two profiles are of different devices: /device:TPU:14 before, /device:TPU:28 now
where the time goes in v2:
time: 44.9 us; the launch traced here: 44.8 us
  Pallas kernels  41.7 us (93%)
  local copies, waits for them, and re-layouts  3.01 us (7%)
    pallas_call x1, Pallas kernels, per_device(): pl.pallas_call(functools.partial(kernel, levels, n_rows, n_z), out_shape=...  41.7 us
    unnamed x2, local copies, waits for them, and re-layouts  3.01 us

profile of v2, /device:TPU:28, one launch (start us, length us, event | category | flops | bytes accessed | tf_op | source)
XLA Modules:
  0.0 44.8 jit_solution(16534175487825492102)
XLA Ops:
  0.0 1.3 %copy.4.slot_ref = s32[1,8,2]{2,1,0:T(8,128)} copy(s32[1,8,2]{1,2,0:T(2,128)} %param.5) | data formatting | bytes 128 | tf_op args[2]
  1.3 41.7 %shard_map.37 = f32[512,128]{1,0:T(8,128)} custom-call(s32[1,8,2]{2,1,0:T(8,128)} %copy.4.slot_ref, f32[512,128]{1,0:T(8,128)} %eig_ref.1, f32[1,128,128]{2,1,0:T(8,128)} %wy_ref.1), custom_call_target="tpu_custom_call" | custom-call | tf_op jit(solution)/shard_map/pallas_call | solution.py:319
  43.1 1.7 %copy.6 = f32[512,128]{1,0:T(8,128)} copy(f32[512,128]{1,0:T(8,128)} %shard_map.37) | data formatting | bytes 524288

commit v3 on v2

--- a/solution.py
+++ b/solution.py
@@ -107,8 +107,15 @@
     def to_core(zz, xx):
         return block_copy(zz * 4 + xx * 2 + k, core_partner, send_sem.at[zz * 2 + xx, 1])
 
-    def to_z(at):
-        return block_copy(c, z_mates[at], own_sem.at[at])
+    def to_z(zz):
+        return block_copy(c, zz * 4 + x * 2 + k, own_sem.at[zz])
+
+    def relay_z(zz):
+        @pl.when(z != zz)
+        def _():
+            to_x(zz, x).wait_recv()
+            to_x(zz, x).start()
+            to_core(zz, x).start()
 
     def relay_x(zz):
         to_core(zz, 1 - x).wait_recv()
@@ -158,7 +165,7 @@
 
     def send_half(at):
         level = 2 * at + 1
-        first = slot_ref[0, level, per_level - 1] == 0
+        first = slot_ref[0, per_level - 1, level] == 0
         rows = pl.ds(k * half, half)
         half_send[at] = jnp.where(
             first, wg[level * per_level, rows], wg[level * per_level + 1, rows]
@@ -169,10 +176,12 @@
     pl.semaphore_wait(
         barrier, n_z + 1 + has_above.astype(jnp.int32) + has_below.astype(jnp.int32)
     )
-    for at in range(n_z - 1):
-        to_z(at).start()
     to_x(z, x).start()
     to_core(z, x).start()
+    for far in range(n_z - 1, -1, -1):
+        @pl.when((far != z) & ((far < z) | (z < 2)))
+        def _():
+            to_z(far).start()
 
     @pl.when(jnp.logical_not(has_above))
     def _():
@@ -195,7 +204,7 @@
         return jnp.concatenate([jnp.where(upper, w, zero), jnp.where(upper, zero, w)], axis=1)
 
     def chosen(level, h):
-        first = slot_ref[0, level, h] == 0
+        first = slot_ref[0, h, level] == 0
         return jnp.where(first, wg[level * per_level], wg[level * per_level + 1])
 
     def prepare(sheared, places):
@@ -215,12 +224,14 @@
         new = pair - product(split(projected), (ops[place, 2], ops[place, 3]))
         return new[:, :band], new[:, band:]
 
-    for zz in range(n_z):
-        @pl.when(z != zz)
-        def _():
-            to_x(zz, x).wait_recv()
-            to_x(zz, x).start()
-            to_core(zz, x).start()
+    relay_z(0)
+
+    @pl.when(z >= 2)
+    def _():
+        for far in range(n_z - 1, 2, -1):
+            @pl.when(far > z)
+            def _():
+                to_z(far).start()
 
     relay_x(0)
     wait_core(0)
@@ -229,9 +240,15 @@
     def _():
         send_half(0)
 
+    relay_z(1)
     prepare([chosen(0, 0), chosen(0, 1)], [3, 4])
 
     def both_levels(at, carry):
+        @pl.when(has_above)
+        def _():
+            half_down(at).wait_recv()
+            half_side(at).start()
+
         for h in range(per_level):
             xt[2 * h], xt[2 * h + 1] = reflected(3 + h, xt[2 * h], xt[2 * h + 1])
 
@@ -254,10 +271,12 @@
             def _():
                 send_half(at + 1)
 
-        @pl.when(has_above)
-        def _():
-            half_down(at).wait_recv()
-            half_side(at).start()
+        @pl.when(at < rounds - 2)
+        def _():
+            relay_z(at + 2)
+
+        @pl.when(has_above)
+        def _():
             half_side(at).wait_recv()
 
         odd, even = 2 * at + 1, (2 * at + 2) % levels
@@ -286,8 +305,11 @@
     for i in range(chunks):
         out_ref[i * band : (i + 1) * band, :] = jnp.transpose(xt[i])
 
-    for at in range(n_z - 1):
-        to_z(at).wait_send()
+    for zz in range(n_z):
+        @pl.when(z != zz)
+        def _():
+            to_z(zz).wait_send()
+
     for zz in range(n_z):
         to_x(zz, x).wait_send()
         for xx in range(2):
@@ -333,14 +355,14 @@
             slots,
             pltpu.SemaphoreType.DMA((n_cols,)),
             pltpu.SemaphoreType.DMA((n_cols // 2, 2)),
-            pltpu.SemaphoreType.DMA((n_z - 1,)),
+            pltpu.SemaphoreType.DMA((n_z,)),
             in_order,
             in_order,
             in_order,
             in_order,
         ],
         compiler_params=pltpu.CompilerParams(collective_id=0, has_side_effects=True),
-    )(slot_block, eigvecs, wy_packed)
+    )(jnp.swapaxes(slot_block, 1, 2), eigvecs, wy_packed)
 
 
 def solution(mesh):

time: 44.9 us -> 40.8 us (0.909)
  the two profiles are of different devices: /device:TPU:28 before, /device:TPU:8 now
where the time goes in v3:
time: 40.8 us; the launch traced here: 40.6 us
  Pallas kernels  38.9 us (95%)
  local copies, waits for them, and re-layouts  1.67 us (4%)
    pallas_call x1, Pallas kernels, per_device(): pl.pallas_call(functools.partial(kernel, levels, n_rows, n_z), out_shape=...  38.9 us
    unnamed x1, local copies, waits for them, and re-layouts  1.67 us

profile of v3, /device:TPU:8, one launch (start us, length us, event | category | flops | bytes accessed | tf_op | source)
XLA Modules:
  0.0 40.6 jit_solution(3524106952817003822)
XLA Ops:
  0.0 38.9 %shard_map.37 = f32[512,128]{1,0:T(8,128)} custom-call(s32[1,2,8]{2,1,0:T(2,128)} %bitcast.1, f32[512,128]{1,0:T(8,128)} %eig_ref.1, f32[1,128,128]{2,1,0:T(8,128)} %wy_ref.1), custom_call_target="tpu_custom_call" | custom-call | tf_op jit(solution)/shard_map/pallas_call | solution.py:341
  38.9 1.7 %copy.5 = f32[512,128]{1,0:T(8,128)} copy(f32[512,128]{1,0:T(8,128)} %shard_map.37) | data formatting | bytes 524288

commit v4 on v3

--- a/solution.py
+++ b/solution.py
@@ -218,11 +218,18 @@
             ops[place, 2] = v[0]
             ops[place, 3] = v[1]
 
-    def reflected(place, top, bottom):
-        pair = jnp.concatenate([top, bottom], axis=1)
-        projected = product(split(pair), (ops[place, 0], ops[place, 1]), NT)
-        new = pair - product(split(projected), (ops[place, 2], ops[place, 3]))
-        return new[:, :band], new[:, band:]
+    def reflected(places, pairs):
+        halves = [split(pair) for pair in pairs]
+        projected = [
+            split(product(x, (ops[p, 0], ops[p, 1]), NT)) for p, x in zip(places, halves)
+        ]
+        return [
+            pair - product(y, (ops[p, 2], ops[p, 3]))
+            for p, y, pair in zip(places, projected, pairs)
+        ]
+
+    def window(top, bottom):
+        return jnp.concatenate([top, bottom], axis=1)
 
     relay_z(0)
 
@@ -249,8 +256,9 @@
             half_down(at).wait_recv()
             half_side(at).start()
 
-        for h in range(per_level):
-            xt[2 * h], xt[2 * h + 1] = reflected(3 + h, xt[2 * h], xt[2 * h + 1])
+        upper_new, lower_new = reflected([3, 4], [window(xt[0], xt[1]), window(xt[2], xt[3])])
+        xt[0], xt[1] = upper_new[:, :band], upper_new[:, band:]
+        xt[2], xt[3] = lower_new[:, :band], lower_new[:, band:]
 
         @pl.when(has_above)
         def _():
@@ -284,7 +292,6 @@
             [chosen(odd, 0), chosen(odd, 1), above[at], chosen(even, 0), chosen(even, 1)],
             [0, 1, 2, 3, 4],
         )
-        xt[1], xt[2] = reflected(0, xt[1], xt[2])
 
         @pl.when(has_below)
         def _():
@@ -294,10 +301,17 @@
         def _():
             go_down(at).wait_recv()
 
-        last, _ = reflected(1, xt[chunks - 1], up_recv[at])
-        _, first = reflected(2, down_recv[at], xt[0])
-        xt[chunks - 1] = last
-        xt[0] = jnp.where(has_above, first, xt[0])
+        middle, last, first = reflected(
+            [0, 1, 2],
+            [
+                window(xt[1], xt[2]),
+                window(xt[chunks - 1], up_recv[at]),
+                window(down_recv[at], xt[0]),
+            ],
+        )
+        xt[1], xt[2] = middle[:, :band], middle[:, band:]
+        xt[chunks - 1] = last[:, :band]
+        xt[0] = jnp.where(has_above, first[:, band:], xt[0])
         return carry
 
     lax.fori_loop(0, rounds, both_levels, 0)

time: 40.8 us -> 39.3 us (0.963)
  Pallas kernels: 38.9 us -> 37.4 us
    pallas_call x1, Pallas kernels: 38.9 us -> 37.4 us  [per_device(): pl.pallas_call(functools.partial(kernel, levels, n_rows, n_z), out_shape=...]
where the time goes in v4:
time: 39.3 us; the launch traced here: 39.1 us
  Pallas kernels  37.4 us (95%)
  local copies, waits for them, and re-layouts  1.67 us (4%)
    pallas_call x1, Pallas kernels, per_device(): pl.pallas_call(functools.partial(kernel, levels, n_rows, n_z), out_shape=...  37.4 us
    unnamed x1, local copies, waits for them, and re-layouts  1.67 us

profile of v4, /device:TPU:8, one launch (start us, length us, event | category | flops | bytes accessed | tf_op | source)
XLA Modules:
  0.0 39.1 jit_solution(15315354178553144482)
XLA Ops:
  0.0 37.4 %shard_map.37 = f32[512,128]{1,0:T(8,128)} custom-call(s32[1,2,8]{2,1,0:T(2,128)} %bitcast.1, f32[512,128]{1,0:T(8,128)} %eig_ref.1, f32[1,128,128]{2,1,0:T(8,128)} %wy_ref.1), custom_call_target="tpu_custom_call" | custom-call | tf_op jit(solution)/shard_map/pallas_call | solution.py:355
  37.4 1.7 %copy.5 = f32[512,128]{1,0:T(8,128)} copy(f32[512,128]{1,0:T(8,128)} %shard_map.37) | data formatting | bytes 524288
